TPU v7x, 512 devices: a whole 4x4x16 slice. The times are simulated.
512 devices in a mesh: stops: 256 (over y, x, z), veh: 2 (over core).
Axes of the slice: x: 4, y: 4, z: 16, core: 2. Of those that a mesh axis runs over, the one named last changes fastest.
Arguments:
- customer_features: bfloat16 [1048576, 128], P('stops'), may hold values from -20 to 20, as said below
- customer_loads: int32 [1048576], P('stops'), may hold values from 1 to 8
- truck_limits: int32 [2048], replicated, may hold values from 1536 to 3072
- truck_features: bfloat16 [2048, 128], replicated, may hold values from -20 to 20
- customer_average_matrix: bfloat16 [128, 128], replicated, may hold values from -1.5 to 1.5
- truck_identity_matrix: bfloat16 [128, 128], replicated, may hold values from -0.5 to 0.5
- hidden_offset: float32 [128], replicated, may hold values from -4 to 4
- output_projector: bfloat16 [128, 128], replicated, may hold values from -0.5 to 0.5
Outputs:
- new_vehicles: bfloat16 [2048, 128], P('veh')
Inputs may be any that keep to these rules, and one draw needn't show every extreme that they name: `customer_features`: stop embeddings; stops of one block of 4096 form one region.
All inputs are finite; a program needn't handle non-finite values.
Results may differ from a plain program's by a relative error of at most 0.0085.
Values may be sent and summed in bfloat16 or wider, within the bound.
No kernel may reach another device: no remote copies, remote signals or barrier semaphores. Data moves between devices by JAX's collectives and lax.ppermute only.
A program may use at most 64 MiB of HBM per device.

v0:
```python
import jax
import jax.numpy as jnp
from jax import lax
from jax.sharding import PartitionSpec as P


def joined(part, axis, combine):
    gathered = jax.tree.map(lambda a: lax.all_gather(a, axis), part)

    def take(source):
        return jax.tree.map(lambda a: lax.dynamic_index_in_dim(a, source, 0, False), gathered)

    return lax.fori_loop(
        1, lax.axis_size(axis), lambda source, state: combine(state, take(source)), take(0)
    )


def join_parts(first, second):
    top = jnp.maximum(first[0], second[0])
    total = first[1] * jnp.exp(first[0] - top) + second[1] * jnp.exp(second[0] - top)
    return (top, total)


def row_lse(values):
    top = jnp.max(values, axis=1)
    total = jnp.sum(jnp.exp(values - top[:, None]), axis=1)
    top, total = joined((top, total), "veh", join_parts)
    return top + jnp.log(total)


def update_rows(
    num,
    den,
    own_rows,
    customer_average_matrix,
    truck_identity_matrix,
    hidden_offset,
    output_projector,
):
    centroid = (num / den[:, None]).astype(jnp.bfloat16)
    pre = jnp.dot(centroid, customer_average_matrix, preferred_element_type=jnp.float32)
    pre = (
        pre
        + jnp.dot(own_rows, truck_identity_matrix, preferred_element_type=jnp.float32)
        + hidden_offset[None, :]
    )
    hidden = jax.nn.silu(pre).astype(jnp.bfloat16)
    update = jnp.dot(hidden, output_projector, preferred_element_type=jnp.float32)
    return (own_rows.astype(jnp.float32) + update).astype(jnp.bfloat16)


def on_device(
    customer_features,
    customer_loads,
    truck_limits,
    truck_features,
    customer_average_matrix,
    truck_identity_matrix,
    hidden_offset,
    output_projector,
):
    width = truck_features.shape[1]
    scale = 1.0 / width**0.5
    veh_count = lax.axis_size("veh")
    truck_index = lax.axis_index("veh")
    radius_span = truck_features.shape[0] // veh_count
    my_veh = lax.dynamic_slice_in_dim(truck_features, truck_index * radius_span, radius_span, 0)
    local_capacity = lax.dynamic_slice_in_dim(
        truck_limits, truck_index * radius_span, radius_span, 0
    )
    log_a = jnp.log(customer_loads.astype(jnp.float32))
    target_share_logarithm = jnp.log(local_capacity.astype(jnp.float32))
    scores = jnp.dot(customer_features, my_veh.T, preferred_element_type=jnp.float32) * scale
    f_one = log_a - row_lse(scores)
    col_part = jnp.sum(jnp.exp(f_one[:, None] + scores), axis=0)
    colsum = lax.psum(col_part, "stops")
    g_one = target_share_logarithm - jnp.log(colsum)
    f_two = log_a - row_lse(scores + g_one[None, :])
    plan = jnp.exp(f_two[:, None] + g_one[None, :] + scores).astype(jnp.bfloat16)
    den = jnp.sum(plan, axis=0, dtype=jnp.float32)
    num = lax.dot_general(
        plan, customer_features, (((0,), (0,)), ((), ())), preferred_element_type=jnp.float32
    )
    num, den = lax.psum((num, den), "stops")
    return update_rows(
        num,
        den,
        my_veh,
        customer_average_matrix,
        truck_identity_matrix,
        hidden_offset,
        output_projector,
    )


def solution(mesh):
    placed = (P("stops", None), P("stops"), P(), P(), P(), P(), P(), P())
    return jax.shard_map(
        on_device, mesh=mesh, in_specs=placed, out_specs=P("veh", None), check_vma=False
    )
```

profile of v0, /device:TPU:32, one launch (start us, length us, event | category | flops | bytes accessed | tf_op | source)
XLA Modules:
  0.0 1458.4 jit_solution(17495390267495161967)
XLA Ops:
  6.5 0.0 copy-start
  6.5 0.0 all-reduce.2.cloned.1.call-start
  6.5 1.2 copy-done
  7.8 9.0 multiply_reduce_fusion
  16.8 1.8 all-gather
  18.6 8.5 fusion.1
  27.1 1.8 all-gather.1
  29.0 0.0 copy-done.2
  29.0 8.6 fusion.3
  37.6 690.8 %psum.21 = f32[1024]{0:T(1024)S(1)} all-reduce(f32[1024]{0:T(1024)S(1)} %fusion.3), channel_id=1, replica_groups=mesh['stops'=256,'veh'=2] {'stops'}, use_global_device_ids=true, to_apply=%region_3.4 | all-reduce | flops 1024 | bytes 8192 | tf_op jit(solution)/shard_map/psum | solution.py:76
  728.4 0.0 copy-done.3
  728.5 7.7 fusion.6
  736.2 7.8 exponential_reduce_fusion
  744.0 1.8 all-gather.2
  745.8 2.0 all-gather.3
  747.9 0.0 copy-start.4
  747.9 0.0 copy-start.1
  747.9 0.0 copy-start.5
  747.9 0.0 copy-start.6
  747.9 0.0 copy-start.7
  747.9 8.5 convert_reduce_fusion
  756.4 3.1 fusion.31
  759.5 0.0 all-reduce.2.cloned.1.call-update
  759.5 689.5 %psum.23 = f32[1024]{0:T(1024)S(1)} all-reduce(f32[1024]{0:T(1024)S(1)} %get-tuple-element.27), channel_id=1, replica_groups=mesh['stops'=256,'veh'=2] {'stops'}, use_global_device_ids=true, to_apply=%region_8.9 | all-reduce | flops 1024 | bytes 8192 | tf_op jit(solution)/shard_map/psum | solution.py:84
  1449.0 0.0 all-reduce.2.cloned.1.call-done
  1449.0 0.0 copy-done.4
  1449.0 1.4 fusion.11
  1450.4 0.0 copy-done.1
  1450.4 0.0 copy-done.5
  1450.4 0.0 copy-done.6
  1450.4 0.0 copy-done.7
  1450.4 1.1 fusion.8
  (5 shorter events, 0.1 us)
Async XLA Ops:
  6.5 1.2 copy-start
  6.5 1442.5 %all-reduce.2.cloned.1.call-start = ((), (), s32[]{:S(2)}) async-start(), calls=%async_computation | async-start | bytes 1048576 | tf_op jit(solution)/shard_map/psum | solution.py:84
  7.8 21.2 %copy-start.2 = (s32[4096]{0:T(1024)S(1)}, s32[4096]{0:T(1024)}, u32[]{:S(2)}) copy-start(s32[4096]{0:T(1024)} %param.9) | copy-start | bytes 49156
  18.6 709.8 %copy-start.3 = (s32[2048]{0:T(1024)S(1)}, s32[2048]{0:T(1024)}, u32[]{:S(2)}) copy-start(s32[2048]{0:T(1024)} %param.10) | copy-start | bytes 24580
  747.9 701.2 %copy-start.4 = (bf16[128,128]{1,0:T(8,128)(2,1)S(1)}, bf16[128,128]{1,0:T(8,128)(2,1)}, u32[]{:S(2)}) copy-start(bf16[128,128]{1,0:T(8,128)(2,1)} %param.12) | copy-start | bytes 98308
  747.9 702.5 %copy-start.1 = (bf16[2048,128]{1,0:T(8,128)(2,1)S(1)}, bf16[2048,128]{1,0:T(8,128)(2,1)}, u32[]{:S(2)}) copy-start(bf16[2048,128]{1,0:T(8,128)(2,1)} %param.11) | copy-start | bytes 1572868
  747.9 702.5 %copy-start.5 = (bf16[128,128]{1,0:T(8,128)(2,1)S(1)}, bf16[128,128]{1,0:T(8,128)(2,1)}, u32[]{:S(2)}) copy-start(bf16[128,128]{1,0:T(8,128)(2,1)} %param.15) | copy-start | bytes 98308
  747.9 702.5 %copy-start.6 = (bf16[128,128]{1,0:T(8,128)(2,1)S(1)}, bf16[128,128]{1,0:T(8,128)(2,1)}, u32[]{:S(2)}) copy-start(bf16[128,128]{1,0:T(8,128)(2,1)} %param.13) | copy-start | bytes 98308
  747.9 702.5 %copy-start.7 = (f32[128]{0:T(128)S(1)}, f32[128]{0:T(128)}, u32[]{:S(2)}) copy-start(f32[128]{0:T(128)} %param.14) | copy-start | bytes 1540
Sparse Core Ops, SparseCore 0:
  759.7 383.6 all-reduce.1
where the time goes:
time: 1460 us
  blocking collectives  1390 us (95%)
  other arithmetic  41.2 us (3%)
  matrix products  14.6 us (1%)
    psum x1, blocking collectives, on_device(): colsum = lax.psum(col_part, 'stops')  691 us
    psum x1, blocking collectives, on_device(): num, den = lax.psum((num, den), 'stops')  689 us
  transfers between devices with their start and end apart: 1, of which 0 were waited for; matrix products, arithmetic and copies ran while one was open for 0% of the time, Pallas kernels for 0%

commit v1 on v0

--- a/solution.py
+++ b/solution.py
@@ -73,7 +73,7 @@
     scores = jnp.dot(customer_features, my_veh.T, preferred_element_type=jnp.float32) * scale
     f_one = log_a - row_lse(scores)
     col_part = jnp.sum(jnp.exp(f_one[:, None] + scores), axis=0)
-    colsum = lax.psum(col_part, "stops")
+    colsum = jnp.sum(lax.all_gather(col_part, "stops"), axis=0)
     g_one = target_share_logarithm - jnp.log(colsum)
     f_two = log_a - row_lse(scores + g_one[None, :])
     plan = jnp.exp(f_two[:, None] + g_one[None, :] + scores).astype(jnp.bfloat16)

time: 1460 us -> 961 us (0.66)
  the two profiles are of different devices: /device:TPU:32 before, /device:TPU:0 now
where the time goes in v1:
time: 961 us
  blocking collectives  696 us (72%)
  waiting for transfers between devices  191 us (20%)
  other arithmetic  41.9 us (4%)
  matrix products  14.6 us (2%)
  between operations  13.5 us (1%)
    psum x1, blocking collectives, on_device(): num, den = lax.psum((num, den), 'stops')  689 us
    all_gather x1, waiting for transfers between devices, on_device(): colsum = jnp.sum(lax.all_gather(col_part, 'stops'), axis=0)  191 us
  transfers between devices with their start and end apart: 2, of which 1 were waited for; matrix products, arithmetic and copies ran while one was open for 0% of the time, Pallas kernels for 0%

profile of v1, /device:TPU:0, one launch (start us, length us, event | category | flops | bytes accessed | tf_op | source)
XLA Modules:
  0.0 960.5 jit_solution(4184194626931201981)
XLA Ops:
  6.5 0.0 copy-start
  6.5 0.0 all-gather.7.cloned.1.call-start
  6.5 1.2 copy-done
  7.8 9.0 multiply_reduce_fusion
  16.8 1.8 all-gather
  18.6 8.5 fusion.1
  27.1 1.8 all-gather.1
  29.0 0.0 copy-done.2
  29.0 9.2 fusion.3
  38.2 0.0 all-gather.7.cloned.1.call-update
  38.3 0.2 all-reduce.2.cloned.1.call-start
  38.5 191.0 %all-gather.7.cloned.1.call-done = f32[262144]{0:T(1024)} async-done(((f32[1024]{0:T(1024)}), f32[262144]{0:T(1024)}) %all-gather.7.cloned.1.call-update) | async-done | bytes 1048592 | tf_op jit(solution)/shard_map/all_gather | solution.py:76
  229.5 1.4 reshape.9
  230.9 0.1 reduce_sum.47
  231.0 0.0 copy-done.3
  231.0 7.7 fusion.6
  238.8 7.8 exponential_reduce_fusion
  246.6 1.8 all-gather.3
  248.4 1.8 all-gather.4
  250.3 0.0 copy-start.4
  250.3 0.0 copy-start.1
  250.3 0.0 copy-start.5
  250.3 0.0 copy-start.6
  250.3 0.0 copy-start.7
  250.3 8.5 convert_reduce_fusion
  258.8 3.1 fusion.31
  261.9 0.0 all-reduce.2.cloned.1.call-update
  261.9 689.2 %psum.15 = f32[1024]{0:T(1024)S(1)} all-reduce(f32[1024]{0:T(1024)S(1)} %get-tuple-element.27), channel_id=1, replica_groups=mesh['stops'=256,'veh'=2] {'stops'}, use_global_device_ids=true, to_apply=%region_8.9 | all-reduce | flops 1024 | bytes 8192 | tf_op jit(solution)/shard_map/psum | solution.py:84
  951.1 0.0 all-reduce.2.cloned.1.call-done
  951.2 0.0 copy-done.4
  951.2 1.4 fusion.11
  952.6 1.1 fusion.8
  (9 shorter events, 0.1 us)
Async XLA Ops:
  6.5 1.2 copy-start
  6.5 223.0 %all-gather.7.cloned.1.call-start = ((), (), s32[]{:S(2)}) async-start(), calls=%async_computation.1 | async-start | bytes 1052672 | tf_op jit(solution)/shard_map/all_gather | solution.py:76
  7.8 21.2 %copy-start.2 = (s32[4096]{0:T(1024)S(1)}, s32[4096]{0:T(1024)}, u32[]{:S(2)}) copy-start(s32[4096]{0:T(1024)} %param.9) | copy-start | bytes 49156
  18.6 212.4 %copy-start.3 = (s32[2048]{0:T(1024)S(1)}, s32[2048]{0:T(1024)}, u32[]{:S(2)}) copy-start(s32[2048]{0:T(1024)} %param.10) | copy-start | bytes 24580
  38.3 912.9 %all-reduce.2.cloned.1.call-start = ((), (), s32[]{:S(2)}) async-start(), calls=%async_computation | async-start | bytes 1048576 | tf_op jit(solution)/shard_map/psum | solution.py:84
  250.3 700.9 %copy-start.4 = (bf16[128,128]{1,0:T(8,128)(2,1)S(1)}, bf16[128,128]{1,0:T(8,128)(2,1)}, u32[]{:S(2)}) copy-start(bf16[128,128]{1,0:T(8,128)(2,1)} %param.12) | copy-start | bytes 98308
  250.3 702.3 %copy-start.1 = (bf16[2048,128]{1,0:T(8,128)(2,1)S(1)}, bf16[2048,128]{1,0:T(8,128)(2,1)}, u32[]{:S(2)}) copy-start(bf16[2048,128]{1,0:T(8,128)(2,1)} %param.11) | copy-start | bytes 1572868
  250.3 702.3 %copy-start.5 = (bf16[128,128]{1,0:T(8,128)(2,1)S(1)}, bf16[128,128]{1,0:T(8,128)(2,1)}, u32[]{:S(2)}) copy-start(bf16[128,128]{1,0:T(8,128)(2,1)} %param.15) | copy-start | bytes 98308
  250.3 702.3 %copy-start.6 = (bf16[128,128]{1,0:T(8,128)(2,1)S(1)}, bf16[128,128]{1,0:T(8,128)(2,1)}, u32[]{:S(2)}) copy-start(bf16[128,128]{1,0:T(8,128)(2,1)} %param.13) | copy-start | bytes 98308
  250.3 702.3 %copy-start.7 = (f32[128]{0:T(128)S(1)}, f32[128]{0:T(128)}, u32[]{:S(2)}) copy-start(f32[128]{0:T(128)} %param.14) | copy-start | bytes 1540
Sparse Core Ops, SparseCore 0:
  38.4 191.1 all-gather.6
  262.1 388.6 all-reduce.1
